TPU v7x, 256 devices: a whole 4x4x8 slice. The times are simulated.
256 devices in a mesh: own: 32 (over y, x, core), row: 8 (over z).
Axes of the slice: x: 4, y: 4, z: 8, core: 2. Of those that a mesh axis runs over, the one named last changes fastest.
Arguments:
- weights: float32 [32, 8, 128, 2048], P('own', None, 'row'), may hold values from -200 to 200
- first_moment: float32 [32, 8, 128, 2048], P('own', None, 'row'), may hold values from -20 to 20
- second_moment: float32 [32, 8, 128, 2048], P('own', None, 'row'), may hold values from 0.002 to 0.05
- gradient: bfloat16 [32, 8, 128, 2048], P('own', None, 'row'), may hold values from -0.59765625 to 0.59765625
- owner: int32 [127], replicated, may hold values from 0 to 31, as said below
Outputs:
- new_weights: float32 [32, 8, 128, 2048], P('own', None, 'row')
- new_first: float32 [32, 8, 128, 2048], P('own', None, 'row')
- new_second: float32 [32, 8, 128, 2048], P('own', None, 'row')
- low_weights: bfloat16 [32, 8, 128, 2048], P('own')
- weight_norms: float32 [14], replicated
- update_norms: float32 [14], replicated
- trust_ratios: float32 [14], replicated
Inputs may be any that keep to these rules, and one draw needn't show every extreme that they name: No owner group holds more than 8 tiles, and one holds exactly 8.
All inputs are finite; a program needn't handle non-finite values.
Results may differ from a plain program's by a relative error of at most 0.0004.
Values may be sent and summed in bfloat16 or wider, within the bound.
A program may use at most 128 MiB of HBM per device.

v0:
```python
import jax
import jax.numpy as jnp
import numpy as np
from jax import lax
from jax.sharding import PartitionSpec as P

QW = 4096
KVW = 512
NEXP = 128
FF = 768
EW = 3
TILE = 128
MATS = 14


DECAY = 0.1
STEP_SIZE = 0.05
EPSILON = 1e-06


def matrix_table():
    counts = [QW // TILE, KVW // TILE, KVW // TILE, QW // TILE, NEXP // TILE] + [FF // TILE] * (
        3 * EW
    )
    return np.repeat(np.arange(len(counts)), counts).astype(np.int32)


def slot_select(owner, owners_count, slot_count, matrices):
    tile_table = jnp.asarray(matrix_table())
    owner_hit = (owner[:, None] == jnp.arange(owners_count, dtype=jnp.int32)[None, :]).astype(
        jnp.int32
    )
    tile_rank = jnp.sum((jnp.cumsum(owner_hit, 0) - owner_hit) * owner_hit, 1)
    slot_hit = tile_rank[:, None] == jnp.arange(slot_count, dtype=jnp.int32)[None, :]
    matrix_hit = tile_table[:, None] == jnp.arange(matrices, dtype=jnp.int32)[None, :]
    owner_bool = owner_hit > 0
    joined = (
        owner_bool[:, :, None, None] & slot_hit[:, None, :, None] & matrix_hit[:, None, None, :]
    )
    return jnp.any(joined, axis=0).astype(jnp.float32)


def shards(weights, first_moment, second_moment, gradient, owner):
    slot_count = weights.shape[1]
    select_all = slot_select(owner, lax.axis_size("own"), slot_count, MATS)
    select = lax.dynamic_index_in_dim(select_all, lax.axis_index("own"), 0, keepdims=False)
    used = jnp.sum(select, 1)[None, :, None, None]
    grad_wide = gradient.astype(jnp.float32)
    moment_one = 0.5 * first_moment + 0.5 * grad_wide
    moment_two = 0.5 * second_moment + 0.5 * grad_wide * grad_wide
    direction = moment_one / (jnp.sqrt(moment_two) + EPSILON) + DECAY * weights
    weight_sq = jnp.sum(weights * weights, axis=(2, 3))[0]
    update_sq = jnp.sum(direction * direction, axis=(2, 3))[0]
    weight_part = jnp.sum(select * weight_sq[:, None], 0)
    update_part = jnp.sum(select * update_sq[:, None], 0)
    weight_total, update_total = lax.psum((weight_part, update_part), ("own", "row"))
    weight_norms = jnp.sqrt(weight_total)
    update_norms = jnp.sqrt(update_total)
    trust_ratios = weight_norms / (update_norms + EPSILON)
    slot_ratio = jnp.sum(select * trust_ratios[None, :], 1)[None, :, None, None]
    new_weights = used * (weights - STEP_SIZE * slot_ratio * direction)
    low_weights = lax.all_gather(new_weights.astype(jnp.bfloat16), "row", axis=2, tiled=True)
    new_first = used * moment_one
    new_second = used * moment_two
    return (
        new_weights,
        new_first,
        new_second,
        low_weights,
        weight_norms,
        update_norms,
        trust_ratios,
    )


def solution(mesh):
    placed = (
        P("own", None, "row", None),
        P("own", None, "row", None),
        P("own", None, "row", None),
        P("own", None, "row", None),
        P(),
    )
    return jax.shard_map(
        shards,
        mesh=mesh,
        in_specs=placed,
        out_specs=(
            P("own", None, "row", None),
            P("own", None, "row", None),
            P("own", None, "row", None),
            P("own", None, None, None),
            P(),
            P(),
            P(),
        ),
        check_vma=False,
    )
```

profile of v0, /device:TPU:2, one launch (start us, length us, event | category | flops | bytes accessed | tf_op | source)
XLA Modules:
  0.0 166.6 jit_solution(3595493397532116743)
XLA Ops:
  7.2 0.0 copy-start
  7.2 0.0 all-gather.2.cloned.1.call-start
  7.2 0.7 iota_compare_fusion.1
  8.0 0.7 fusion.4
  8.7 0.1 copy.13
  8.8 0.2 reduce_window_sum.11
  9.0 0.8 select_reduce_fusion
  9.9 7.7 %and_reduce_fusion = pred[32,8,14]{1,2,0:T(8,128)(4,1)S(1)} fusion(pred[127,14]{0,1:T(8,128)(4,1)S(1)} %iota_compare_fusion.1, pred[127,32,8]{0,2,1:T(8,128)(4,1)S(1)} %broadcast_and_fusion), kind=kLoop, calls=%fused_computation | loop fusion | flops 906752 | bytes 37874 | tf_op jit(solution)/shard_map/reduce_or | solution.py:40
  17.7 0.1 copy.14
  17.7 4.3 %multiply_reduce_fusion = (f32[8]{0:T(128)S(1)}, f32[1,8,16,2048]{3,2,1,0:T(8,128)S(1)}, f32[1,8,16,2048]{3,2,1,0:T(8,128)}, f32[1,8,16,2048]{3,2,1,0:T(8,128)}, f32[8]{0:T(128)S(1)}) fusion(f32[1,8,16,2048]{3,2,1,0:T(8,128)} %param.6, f32[1,8,16,2048]{3,2,1,0:T(8,128)} %param.8, bf16[1,8,16,2048]{3,2,1,0:T(8,128)(2,1)} %param.9, ...), kind=kLoop, calls=%fused_computation.5 | loop fusion | flops 4456432 | bytes 6815840 | tf_op jit(solution)/shard_map/reduce_sum | solution.py:53
  22.1 0.1 fusion.6
  22.2 78.7 %all-reduce = (f32[14]{0:T(128)S(1)}, f32[14]{0:T(128)S(1)}) all-reduce(f32[14]{0:T(128)S(1)} %get-tuple-element.8, f32[14]{0:T(128)S(1)} %get-tuple-element.7), channel_id=1, replica_groups=mesh['own'=32,'row'=8] {'own','row'}, use_global_device_ids=true, to_apply=%region_6.7 | all-reduce | flops 28 | bytes 224 | tf_op jit(solution)/shard_map/psum | solution.py:56
  100.8 0.5 add_divide_fusion
  101.4 0.0 copy-start.1
  101.4 0.1 fusion.7
  101.5 0.0 copy-done
  101.5 1.4 fusion.9
  102.9 0.0 all-gather.2.cloned.1.call-update
  102.9 52.0 %all-gather.2.cloned.1.call-done = bf16[1,8,128,2048]{3,2,1,0:T(8,128)(2,1)} async-done(((bf16[1,8,16,2048]{3,2,1,0:T(8,128)(2,1)}), bf16[1,8,128,2048]{3,2,1,0:T(8,128)(2,1)}) %all-gather.2.cloned.1.call-update) | async-done | bytes 4194320 | tf_op jit(solution)/shard_map/all_gather | solution.py:62
  155.0 4.8 %copy.16 = bf16[1,8,128,2048]{3,2,1,0:T(8,128)(2,1)} copy(bf16[1,8,128,2048]{3,2,1,0:T(8,128)(2,1)} %all-gather.2.cloned.1.call-done) | data formatting | bytes 8388608
  159.8 0.0 copy-done.1
  (5 shorter events, 0.1 us)
Async XLA Ops:
  7.2 94.3 %copy-start = (f32[1,8,16,2048]{3,2,1,0:T(8,128)S(1)}, f32[1,8,16,2048]{3,2,1,0:T(8,128)}, u32[]{:S(2)}) copy-start(f32[1,8,16,2048]{3,2,1,0:T(8,128)} %param.6) | copy-start | bytes 3145732
  7.2 147.8 %all-gather.2.cloned.1.call-start = ((), (), s32[]{:S(2)}) async-start(), calls=%async_computation | async-start | bytes 4718592 | tf_op jit(solution)/shard_map/all_gather | solution.py:62
  101.4 58.4 %copy-start.1 = (f32[14]{0:T(128)}, f32[14]{0:T(128)S(1)}, u32[]{:S(2)}) copy-start(f32[14]{0:T(128)S(1)} %get-tuple-element.36) | copy-start | bytes 172
Sparse Core Ops, SparseCore 0:
  103.1 51.8 all-gather.1
where the time goes:
time: 168 us; the launch traced here: 167 us
  blocking collectives  78.7 us (47%)
  waiting for transfers between devices  52 us (31%)
  other arithmetic  16.8 us (10%)
  between operations  14.1 us (8%)
  local copies, waits for them, and re-layouts  4.96 us (3%)
    psum x1, blocking collectives, shards(): lax.psum((weight_part, update_part), ('own', 'row'))  78.7 us
    all_gather x1, waiting for transfers between devices, shards(): lax.all_gather(new_weights.astype(jnp.bfloat16), 'row', axis=2, tiled=True)  52 us
    reduce_or x1, other arithmetic, slot_select(): return jnp.any(joined, axis=0).astype(jnp.float32)  7.73 us
    unnamed x5, local copies, waits for them, and re-layouts  4.8 us
    reduce_sum x1, other arithmetic, shards(): update_sq = jnp.sum(direction * direction, axis=(2, 3))[0]  4.33 us
  transfers between devices with their start and end apart: 1, of which 1 were waited for; matrix products, arithmetic and copies ran while one was open for 0% of the time, Pallas kernels for 0%

commit v1 on v0

v1 whole, which is shorter than its diff:
```python
import functools

import jax
import jax.numpy as jnp
import numpy as np
from jax import lax
from jax.experimental import pallas as pl
from jax.experimental.pallas import tpu as pltpu
from jax.sharding import PartitionSpec as P

QW = 4096
KVW = 512
NEXP = 128
FF = 768
EW = 3
TILE = 128
MATS = 14

DECAY = 0.1
STEP_SIZE = 0.05
EPSILON = 1e-06

MESH = pl.DeviceIdType.MESH
HALF = 64
CHUNK = 512


def matrix_bounds():
    counts = [QW // TILE, KVW // TILE, KVW // TILE, QW // TILE, NEXP // TILE] + [FF // TILE] * (
        3 * EW
    )
    ends = np.cumsum(counts)
    return [(int(e - c), int(e)) for c, e in zip(counts, ends)]


def select_rows(owner, me, slots):
    tiles = owner.shape[1]
    hit = jnp.broadcast_to((owner == me).astype(jnp.float32), (8, tiles))
    before = (
        lax.broadcasted_iota(jnp.int32, (tiles, tiles), 0)
        < lax.broadcasted_iota(jnp.int32, (tiles, tiles), 1)
    ).astype(jnp.float32)
    rank = jnp.dot(hit, before, preferred_element_type=jnp.float32)
    slot = lax.broadcasted_iota(jnp.int32, (slots, tiles), 0).astype(jnp.float32)
    slot_hit = jnp.where(rank == slot, hit, 0.0)
    lane = lax.broadcasted_iota(jnp.int32, (1, 128), 1) % HALF
    first = jnp.full((1, 128), 1 << 20, jnp.int32)
    last = jnp.zeros((1, 128), jnp.int32)
    for k, (a, b) in enumerate(matrix_bounds()):
        first = jnp.where(lane == k, a, first)
        last = jnp.where(lane == k, b, last)
    tile = lax.broadcasted_iota(jnp.int32, (tiles, 128), 0)
    table = ((tile >= first) & (tile < last)).astype(jnp.float32)
    return jnp.dot(slot_hit, table, preferred_element_type=jnp.float32)


def fold(x):
    x = x[0:8, :] + x[8:16, :]
    out = x[:, 0:128]
    for i in range(1, CHUNK // 128):
        out = out + x[:, i * 128 : (i + 1) * 128]
    return out


def kernel(
    owns, rows,
    w_hbm, f_hbm, s_hbm, g_hbm, owner_ref,
    nw_hbm, nf_hbm, ns_hbm, low_hbm, wn_ref, un_ref, tr_ref,
    wv, fv, sv, gv, dv, gath, used_b, ratio_b, sw, su, abuf, bbuf,
    in_sem, out_sem, gat_sem, a_sem, b_sem, rs_sem, rr_sem, ls_sem, lr_sem,
):
    own = lax.axis_index("own")
    z = lax.axis_index("row")
    slots, depth, width = wv.shape

    barrier = pltpu.get_barrier_semaphore()

    @pl.loop(1, owns)
    def _(p):
        pl.semaphore_signal(barrier, inc=1, device_id=(lax.rem(own + p, owns), z), device_id_type=MESH)

    @pl.loop(1, rows)
    def _(p):
        pl.semaphore_signal(barrier, inc=1, device_id=(own, lax.rem(z + p, rows)), device_id_type=MESH)

    def loads(c):
        return [
            pltpu.make_async_copy(src.at[0, c], dst.at[c], in_sem.at[i, c])
            for i, (src, dst) in enumerate(((w_hbm, wv), (f_hbm, fv), (s_hbm, sv), (g_hbm, gv)))
        ]

    @pl.loop(0, slots)
    def _(c):
        for copy in loads(c):
            copy.start()

    select = select_rows(owner_ref[...], own, slots)
    lane = lax.broadcasted_iota(jnp.int32, (1, 128), 1)
    lower = lane < HALF
    used = jnp.sum(jnp.where(lower, select, 0.0), axis=1, keepdims=True)
    used_b[...] = jnp.broadcast_to(used, used_b.shape)

    def stores(c):
        return [
            pltpu.make_async_copy(fv.at[c], nf_hbm.at[0, c], out_sem.at[0, c]),
            pltpu.make_async_copy(sv.at[c], ns_hbm.at[0, c], out_sem.at[1, c]),
        ]

    @pl.loop(0, slots)
    def _(c):
        for copy in loads(c):
            copy.wait()
        keep = used_b[pl.ds(c, 1), :]
        aw = jnp.zeros((8, 128), jnp.float32)
        au = jnp.zeros((8, 128), jnp.float32)
        for j in range(width // CHUNK):
            cols = slice(j * CHUNK, (j + 1) * CHUNK)
            w = wv[c, :, cols]
            g = gv[c, :, cols].astype(jnp.float32)
            m1 = 0.5 * fv[c, :, cols] + 0.5 * g
            m2 = 0.5 * sv[c, :, cols] + 0.5 * g * g
            d = m1 / (jnp.sqrt(m2) + EPSILON) + DECAY * w
            fv[c, :, cols] = keep * m1
            sv[c, :, cols] = keep * m2
            dv[c, :, cols] = d
            aw = aw + fold(w * w)
            au = au + fold(d * d)
        sw[c] = aw
        su[c] = au
        for copy in stores(c):
            copy.start()

    weight_sq = jnp.sum(jnp.sum(sw[...], axis=1), axis=1, keepdims=True)
    update_sq = jnp.sum(jnp.sum(su[...], axis=1), axis=1, keepdims=True)
    part = jnp.sum(select * jnp.where(lower, weight_sq, update_sq), axis=0, keepdims=True)
    abuf[pl.ds(own, 1)] = part.reshape(1, 1, 128)

    pl.semaphore_wait(barrier, owns + rows - 2)

    def plane(p):
        return pltpu.make_async_remote_copy(
            src_ref=abuf.at[own], dst_ref=abuf.at[own],
            send_sem=a_sem.at[0], recv_sem=a_sem.at[1],
            device_id=(lax.rem(own + p, owns), z), device_id_type=MESH,
        )

    def line(p):
        return pltpu.make_async_remote_copy(
            src_ref=bbuf.at[z], dst_ref=bbuf.at[z],
            send_sem=b_sem.at[0], recv_sem=b_sem.at[1],
            device_id=(own, lax.rem(z + p, rows)), device_id_type=MESH,
        )

    @pl.loop(1, owns)
    def _(p):
        plane(p).start()

    whole = abuf.at[pl.ds(0, owns - 1)]
    pltpu.make_async_copy(whole, whole, a_sem.at[1]).wait()
    total = jnp.sum(abuf[...], axis=0)
    bbuf[pl.ds(z, 1)] = total.reshape(1, 1, 128)
    pltpu.make_async_copy(whole, whole, a_sem.at[0]).wait()

    @pl.loop(1, rows)
    def _(p):
        line(p).start()

    whole_b = bbuf.at[pl.ds(0, rows - 1)]
    pltpu.make_async_copy(whole_b, whole_b, b_sem.at[1]).wait()
    norms = jnp.sqrt(jnp.sum(bbuf[...], axis=0))
    updates = pltpu.roll(norms, HALF, 1)
    trust = norms / (updates + EPSILON)
    wn_ref[...] = norms[:, :MATS]
    un_ref[...] = updates[:, :MATS]
    tr_ref[...] = trust[:, :MATS]
    ratio = jnp.sum(jnp.where(lower, select * trust, 0.0), axis=1, keepdims=True)
    ratio_b[...] = jnp.broadcast_to(STEP_SIZE * ratio, ratio_b.shape)

    right, left = lax.rem(z + 1, rows), lax.rem(z + rows - 1, rows)

    def hop(c, h, to_right):
        src = lax.rem(z + rows - h, rows) if to_right else lax.rem(z + h, rows)
        block = gath.at[c, pl.ds(pl.multiple_of(src * depth, depth), depth)]
        send, recv = (rs_sem, rr_sem) if to_right else (ls_sem, lr_sem)
        return pltpu.make_async_remote_copy(
            src_ref=block, dst_ref=block,
            send_sem=send.at[h, c], recv_sem=recv.at[h, c],
            device_id=(own, right if to_right else left), device_id_type=MESH,
        )

    def arrival(c, h, to_right):
        src = lax.rem(z + rows - h - 1, rows) if to_right else lax.rem(z + h + 1, rows)
        block = gath.at[c, pl.ds(pl.multiple_of(src * depth, depth), depth)]
        recv = rr_sem if to_right else lr_sem
        pltpu.make_async_copy(block, block, recv.at[h, c]).wait()
        return src, block

    def keep_block(c, src, block, h, side):
        return pltpu.make_async_copy(
            block, low_hbm.at[0, c, pl.ds(pl.multiple_of(src * depth, depth), depth)], gat_sem.at[side, h, c]
        )

    mine = pl.multiple_of(z * depth, depth)

    @pl.loop(0, slots)
    def _(c):
        keep = used_b[pl.ds(c, 1), :]
        rate = ratio_b[pl.ds(c, 1), :]
        for j in range(width // CHUNK):
            cols = slice(j * CHUNK, (j + 1) * CHUNK)
            new = keep * (wv[c, :, cols] - rate * dv[c, :, cols])
            wv[c, :, cols] = new
            gath[c, pl.ds(mine, depth), cols] = new.astype(jnp.bfloat16)
        hop(c, 0, True).start()
        hop(c, 0, False).start()
        pltpu.make_async_copy(wv.at[c], nw_hbm.at[0, c], out_sem.at[2, c]).start()
        keep_block(c, z, gath.at[c, pl.ds(mine, depth)], 0, 0).start()

    half = slots // 2
    far = rows // 2
    for h in range(far):
        last = h == far - 1
        for to_right, lo, hi in ((True, 0, half if last else slots), (False, half if last else 0, slots)):
            @pl.loop(lo, hi)
            def _(c):
                src, block = arrival(c, h, to_right)
                if h + 1 < far - 1:
                    hop(c, h + 1, to_right).start()
                elif h + 1 == far - 1:
                    @pl.when((c < half) if to_right else (c >= half))
                    def _():
                        hop(c, h + 1, to_right).start()
                keep_block(c, src, block, h + 1, 0 if to_right else 1).start()

    @pl.loop(0, slots)
    def _(c):
        for copy in stores(c):
            copy.wait()
        pltpu.make_async_copy(wv.at[c], nw_hbm.at[0, c], out_sem.at[2, c]).wait()
        keep_block(c, z, gath.at[c, pl.ds(mine, depth)], 0, 0).wait()

    for h in range(far):
        last = h == far - 1
        for to_right, lo, hi in ((True, 0, half if last else slots), (False, half if last else 0, slots)):
            @pl.loop(lo, hi)
            def _(c):
                src = lax.rem(z + rows - h - 1, rows) if to_right else lax.rem(z + h + 1, rows)
                block = gath.at[c, pl.ds(pl.multiple_of(src * depth, depth), depth)]
                keep_block(c, src, block, h + 1, 0 if to_right else 1).wait()
                hop(c, h, to_right).wait_send()

    pltpu.make_async_copy(whole_b, whole_b, b_sem.at[0]).wait()


def shards(owns, rows, weights, first_moment, second_moment, gradient, owner):
    _, slots, depth, width = weights.shape
    any_space = pl.BlockSpec(memory_space=pl.ANY)
    vmem = pl.BlockSpec(memory_space=pltpu.VMEM)
    far = rows // 2
    f32 = jnp.float32
    wide = jax.ShapeDtypeStruct(weights.shape, f32)
    tiny = jax.ShapeDtypeStruct((1, MATS), f32)
    dma = pltpu.SemaphoreType.DMA
    nw, nf, ns, low, wn, un, tr = pl.pallas_call(
        functools.partial(kernel, owns, rows),
        out_shape=(
            wide, wide, wide,
            jax.ShapeDtypeStruct((1, slots, depth * rows, width), jnp.bfloat16),
            tiny, tiny, tiny,
        ),
        in_specs=[any_space] * 4 + [vmem],
        out_specs=(any_space,) * 4 + (vmem,) * 3,
        scratch_shapes=[
            pltpu.VMEM((slots, depth, width), f32),
            pltpu.VMEM((slots, depth, width), f32),
            pltpu.VMEM((slots, depth, width), f32),
            pltpu.VMEM((slots, depth, width), jnp.bfloat16),
            pltpu.VMEM((slots, depth, width), f32),
            pltpu.VMEM((slots, depth * rows, width), jnp.bfloat16),
            pltpu.VMEM((slots, CHUNK), f32),
            pltpu.VMEM((slots, CHUNK), f32),
            pltpu.VMEM((slots, 8, 128), f32),
            pltpu.VMEM((slots, 8, 128), f32),
            pltpu.VMEM((owns, 1, 128), f32),
            pltpu.VMEM((rows, 1, 128), f32),
            dma((4, slots)),
            dma((3, slots)),
            dma((2, far + 1, slots)),
            dma((2,)),
            dma((2,)),
            dma((far, slots)),
            dma((far, slots)),
            dma((far, slots)),
            dma((far, slots)),
        ],
        compiler_params=pltpu.CompilerParams(
            collective_id=0, has_side_effects=True, vmem_limit_bytes=24 << 20
        ),
    )(weights, first_moment, second_moment, gradient, owner.reshape(1, -1))
    return nw, nf, ns, low, wn.reshape(MATS), un.reshape(MATS), tr.reshape(MATS)


def solution(mesh):
    placed = P("own", None, "row", None)
    return jax.shard_map(
        functools.partial(shards, mesh.shape["own"], mesh.shape["row"]),
        mesh=mesh,
        in_specs=(placed, placed, placed, placed, P()),
        out_specs=(placed, placed, placed, P("own", None, None, None), P(), P(), P()),
        check_vma=False,
    )
```

time: 168 us -> 82.5 us (0.49)
  blocking collectives: 78.7 us -> 0 us
  Pallas kernels: 0 us -> 69.7 us
  waiting for transfers between devices: 52 us -> 0 us
  other arithmetic: 16.8 us -> 0 us
  between operations: 14.1 us -> 0.66 us
  local copies, waits for them, and re-layouts: 4.96 us -> 11.8 us
    psum x1 -> x0, blocking collectives: 78.7 us -> none  [shards(): lax.psum((weight_part, update_part), ('own', 'row'))]
    pallas_call x0 -> x1, Pallas kernels: none -> 69.7 us  [shards(): pl.pallas_call(functools.partial(kernel, owns, rows), out_shape=(wide, wi...]
    all_gather x1 -> x0, waiting for transfers between devices: 52 us -> none  [shards(): lax.all_gather(new_weights.astype(jnp.bfloat16), 'row', axis=2, tiled=True)]
    reduce_or x1 -> x0, other arithmetic: 7.73 us -> none  [slot_select(): return jnp.any(joined, axis=0).astype(jnp.float32)]
    unnamed x5 -> x17, local copies, waits for them, and re-layouts: 4.8 us -> 11.8 us
    reduce_sum x5 -> x0, other arithmetic: 5.4 us -> none  [the longest x1 4.33 us: shards(): update_sq = jnp.sum(direction * direction, axis=(2, 3))[0]]
  transfers between devices with their start and end apart: 1 -> 0, of which waited for: 1 -> 0; matrix products, arithmetic and copies ran while one was open for 0% -> 0% of each run, Pallas kernels for 0% -> 0%
where the time goes in v1:
time: 82.5 us; the launch traced here: 82.2 us
  Pallas kernels  69.7 us (84%)
  local copies, waits for them, and re-layouts  11.8 us (14%)
    pallas_call x1, Pallas kernels, shards(): pl.pallas_call(functools.partial(kernel, owns, rows), out_shape=(wide, wi...  69.7 us
    unnamed x17, local copies, waits for them, and re-layouts  11.8 us

profile of v1, /device:TPU:2, one launch (start us, length us, event | category | flops | bytes accessed | tf_op | source)
XLA Modules:
  0.0 82.2 jit_solution(17787773208549892221)
XLA Ops:
  0.6 0.0 copy-start
  0.6 1.2 %copy-done = f32[1,8,16,2048]{3,2,1,0:T(8,128)S(1)} copy-done((f32[1,8,16,2048]{3,2,1,0:T(8,128)S(1)}, f32[1,8,16,2048]{3,2,1,0:T(8,128)}, u32[]{:S(2)}) %copy-start) | copy-done | bytes 1048600
  1.9 0.0 copy-start.1
  1.9 1.2 %copy-done.1 = f32[1,8,16,2048]{3,2,1,0:T(8,128)S(1)} copy-done((f32[1,8,16,2048]{3,2,1,0:T(8,128)S(1)}, f32[1,8,16,2048]{3,2,1,0:T(8,128)}, u32[]{:S(2)}) %copy-start.1) | copy-done | bytes 1048600
  3.1 0.0 copy-start.2
  3.1 1.2 %copy-done.2 = f32[1,8,16,2048]{3,2,1,0:T(8,128)S(1)} copy-done((f32[1,8,16,2048]{3,2,1,0:T(8,128)S(1)}, f32[1,8,16,2048]{3,2,1,0:T(8,128)}, u32[]{:S(2)}) %copy-start.2) | copy-done | bytes 1048600
  4.3 0.0 copy-start.3
  4.3 1.0 %copy-done.3 = bf16[1,8,16,2048]{3,2,1,0:T(8,128)(2,1)S(1)} copy-done((bf16[1,8,16,2048]{3,2,1,0:T(8,128)(2,1)S(1)}, bf16[1,8,16,2048]{3,2,1,0:T(8,128)(2,1)}, u32[]{:S(2)}) %copy-start.3) | copy-done | bytes 524312
  5.4 0.0 copy-start.4
  5.4 0.7 copy-done.4
  6.0 69.7 %shard_map.108 = (f32[1,8,16,2048]{3,2,1,0:T(8,128)S(1)}, f32[1,8,16,2048]{3,2,1,0:T(8,128)S(1)}, f32[1,8,16,2048]{3,2,1,0:T(8,128)S(1)}, bf16[1,8,128,2048]{3,2...) custom-call(f32[1,8,16,2048]{3,2,1,0:T(8,128)S(1)} %copy-done, ...), custom_call_target="tpu_custom_call" | custom-call | tf_op jit(solution)/shard_map/pallas_call | solution.py:264
  75.7 1.0 %copy.19 = f32[1,8,16,2048]{3,2,1,0:T(8,128)} copy(f32[1,8,16,2048]{3,2,1,0:T(8,128)S(1)} %get-tuple-element.28) | data formatting | bytes 2097152
  76.7 1.0 %copy.20 = f32[1,8,16,2048]{3,2,1,0:T(8,128)} copy(f32[1,8,16,2048]{3,2,1,0:T(8,128)S(1)} %get-tuple-element.29) | data formatting | bytes 2097152
  77.7 1.0 %copy.21 = f32[1,8,16,2048]{3,2,1,0:T(8,128)} copy(f32[1,8,16,2048]{3,2,1,0:T(8,128)S(1)} %get-tuple-element.30) | data formatting | bytes 2097152
  78.7 2.0 %copy.22 = bf16[1,8,128,2048]{3,2,1,0:T(8,128)(2,1)} copy(bf16[1,8,128,2048]{3,2,1,0:T(8,128)(2,1)S(1)} %get-tuple-element.31) | data formatting | bytes 8388608
  80.7 0.5 copy.23
  81.2 0.5 copy.24
  81.7 0.5 copy.25
Async XLA Ops:
  0.6 1.2 %copy-start = (f32[1,8,16,2048]{3,2,1,0:T(8,128)S(1)}, f32[1,8,16,2048]{3,2,1,0:T(8,128)}, u32[]{:S(2)}) copy-start(f32[1,8,16,2048]{3,2,1,0:T(8,128)} %w_hbm.1) | copy-start | bytes 3145732
  1.9 1.2 %copy-start.1 = (f32[1,8,16,2048]{3,2,1,0:T(8,128)S(1)}, f32[1,8,16,2048]{3,2,1,0:T(8,128)}, u32[]{:S(2)}) copy-start(f32[1,8,16,2048]{3,2,1,0:T(8,128)} %f_hbm.1) | copy-start | bytes 3145732
  3.1 1.2 %copy-start.2 = (f32[1,8,16,2048]{3,2,1,0:T(8,128)S(1)}, f32[1,8,16,2048]{3,2,1,0:T(8,128)}, u32[]{:S(2)}) copy-start(f32[1,8,16,2048]{3,2,1,0:T(8,128)} %s_hbm.1) | copy-start | bytes 3145732
  4.3 1.0 %copy-start.3 = (bf16[1,8,16,2048]{3,2,1,0:T(8,128)(2,1)S(1)}, bf16[1,8,16,2048]{3,2,1,0:T(8,128)(2,1)}, u32[]{:S(2)}) copy-start(bf16[1,8,16,2048]{3,2,1,0:T(8,128)(2,1)} %g_hbm.1) | copy-start | bytes 1572868
  5.4 0.7 copy-start.4

commit v2 on v1

--- a/solution.py
+++ b/solution.py
@@ -64,10 +64,10 @@
 
 def kernel(
     owns, rows,
-    w_hbm, f_hbm, s_hbm, g_hbm, owner_ref,
-    nw_hbm, nf_hbm, ns_hbm, low_hbm, wn_ref, un_ref, tr_ref,
-    wv, fv, sv, gv, dv, gath, used_b, ratio_b, sw, su, abuf, bbuf,
-    in_sem, out_sem, gat_sem, a_sem, b_sem, rs_sem, rr_sem, ls_sem, lr_sem,
+    w_hbm, f_hbm, s_hbm, g_hbm, owner_hbm,
+    nw, nf, ns, low, wn_ref, un_ref, tr_ref,
+    wv, fv, sv, gv, dv, owner_ref, used_b, ratio_b, sw, su, abuf, bbuf,
+    in_sem, owner_sem, a_sem, b_sem, rs_sem, rr_sem, ls_sem, lr_sem,
 ):
     own = lax.axis_index("own")
     z = lax.axis_index("row")
@@ -89,22 +89,20 @@
             for i, (src, dst) in enumerate(((w_hbm, wv), (f_hbm, fv), (s_hbm, sv), (g_hbm, gv)))
         ]
 
+    owner_load = pltpu.make_async_copy(owner_hbm, owner_ref, owner_sem)
+    owner_load.start()
+
     @pl.loop(0, slots)
     def _(c):
         for copy in loads(c):
             copy.start()
 
+    owner_load.wait()
     select = select_rows(owner_ref[...], own, slots)
     lane = lax.broadcasted_iota(jnp.int32, (1, 128), 1)
     lower = lane < HALF
     used = jnp.sum(jnp.where(lower, select, 0.0), axis=1, keepdims=True)
     used_b[...] = jnp.broadcast_to(used, used_b.shape)
-
-    def stores(c):
-        return [
-            pltpu.make_async_copy(fv.at[c], nf_hbm.at[0, c], out_sem.at[0, c]),
-            pltpu.make_async_copy(sv.at[c], ns_hbm.at[0, c], out_sem.at[1, c]),
-        ]
 
     @pl.loop(0, slots)
     def _(c):
@@ -120,15 +118,13 @@
             m1 = 0.5 * fv[c, :, cols] + 0.5 * g
             m2 = 0.5 * sv[c, :, cols] + 0.5 * g * g
             d = m1 / (jnp.sqrt(m2) + EPSILON) + DECAY * w
-            fv[c, :, cols] = keep * m1
-            sv[c, :, cols] = keep * m2
+            nf[0, c, :, cols] = keep * m1
+            ns[0, c, :, cols] = keep * m2
             dv[c, :, cols] = d
             aw = aw + fold(w * w)
             au = au + fold(d * d)
         sw[c] = aw
         su[c] = au
-        for copy in stores(c):
-            copy.start()
 
     weight_sq = jnp.sum(jnp.sum(sw[...], axis=1), axis=1, keepdims=True)
     update_sq = jnp.sum(jnp.sum(su[...], axis=1), axis=1, keepdims=True)
@@ -180,7 +176,7 @@
 
     def hop(c, h, to_right):
         src = lax.rem(z + rows - h, rows) if to_right else lax.rem(z + h, rows)
-        block = gath.at[c, pl.ds(pl.multiple_of(src * depth, depth), depth)]
+        block = low.at[0, c, pl.ds(pl.multiple_of(src * depth, depth), depth)]
         send, recv = (rs_sem, rr_sem) if to_right else (ls_sem, lr_sem)
         return pltpu.make_async_remote_copy(
             src_ref=block, dst_ref=block,
@@ -190,15 +186,9 @@
 
     def arrival(c, h, to_right):
         src = lax.rem(z + rows - h - 1, rows) if to_right else lax.rem(z + h + 1, rows)
-        block = gath.at[c, pl.ds(pl.multiple_of(src * depth, depth), depth)]
+        block = low.at[0, c, pl.ds(pl.multiple_of(src * depth, depth), depth)]
         recv = rr_sem if to_right else lr_sem
         pltpu.make_async_copy(block, block, recv.at[h, c]).wait()
-        return src, block
-
-    def keep_block(c, src, block, h, side):
-        return pltpu.make_async_copy(
-            block, low_hbm.at[0, c, pl.ds(pl.multiple_of(src * depth, depth), depth)], gat_sem.at[side, h, c]
-        )
 
     mine = pl.multiple_of(z * depth, depth)
 
@@ -209,12 +199,10 @@
         for j in range(width // CHUNK):
             cols = slice(j * CHUNK, (j + 1) * CHUNK)
             new = keep * (wv[c, :, cols] - rate * dv[c, :, cols])
-            wv[c, :, cols] = new
-            gath[c, pl.ds(mine, depth), cols] = new.astype(jnp.bfloat16)
+            nw[0, c, :, cols] = new
+            low[0, c, pl.ds(mine, depth), cols] = new.astype(jnp.bfloat16)
         hop(c, 0, True).start()
         hop(c, 0, False).start()
-        pltpu.make_async_copy(wv.at[c], nw_hbm.at[0, c], out_sem.at[2, c]).start()
-        keep_block(c, z, gath.at[c, pl.ds(mine, depth)], 0, 0).start()
 
     half = slots // 2
     far = rows // 2
@@ -223,60 +211,69 @@
         for to_right, lo, hi in ((True, 0, half if last else slots), (False, half if last else 0, slots)):
             @pl.loop(lo, hi)
             def _(c):
-                src, block = arrival(c, h, to_right)
+                arrival(c, h, to_right)
                 if h + 1 < far - 1:
                     hop(c, h + 1, to_right).start()
                 elif h + 1 == far - 1:
                     @pl.when((c < half) if to_right else (c >= half))
                     def _():
                         hop(c, h + 1, to_right).start()
-                keep_block(c, src, block, h + 1, 0 if to_right else 1).start()
-
-    @pl.loop(0, slots)
-    def _(c):
-        for copy in stores(c):
-            copy.wait()
-        pltpu.make_async_copy(wv.at[c], nw_hbm.at[0, c], out_sem.at[2, c]).wait()
-        keep_block(c, z, gath.at[c, pl.ds(mine, depth)], 0, 0).wait()
 
     for h in range(far):
         last = h == far - 1
         for to_right, lo, hi in ((True, 0, half if last else slots), (False, half if last else 0, slots)):
             @pl.loop(lo, hi)
             def _(c):
-                src = lax.rem(z + rows - h - 1, rows) if to_right else lax.rem(z + h + 1, rows)
-                block = gath.at[c, pl.ds(pl.multiple_of(src * depth, depth), depth)]
-                keep_block(c, src, block, h + 1, 0 if to_right else 1).wait()
                 hop(c, h, to_right).wait_send()
 
     pltpu.make_async_copy(whole_b, whole_b, b_sem.at[0]).wait()
+
+
+def put_out(*refs):
+    held, result, sem = refs[:7], refs[7:14], refs[14]
+    slots = held[0].shape[1]
+    copies = []
+    for i, (src, dst) in enumerate(zip(held, result)):
+        if i == 3:
+            copies += [(src.at[0, c], dst.at[0, c]) for c in range(slots)]
+        elif i < 3:
+            half = slots // 2
+            copies += [(src.at[0, pl.ds(c, half)], dst.at[0, pl.ds(c, half)]) for c in (0, half)]
+        else:
+            copies.append((src, dst))
+    copies = [pltpu.make_async_copy(a, b, sem.at[i]) for i, (a, b) in enumerate(copies)]
+    for copy in copies:
+        copy.start()
+    for copy in copies:
+        copy.wait()
 
 
 def shards(owns, rows, weights, first_moment, second_moment, gradient, owner):
     _, slots, depth, width = weights.shape
-    any_space = pl.BlockSpec(memory_space=pl.ANY)
+    hbm = pl.BlockSpec(memory_space=pltpu.HBM)
     vmem = pl.BlockSpec(memory_space=pltpu.VMEM)
     far = rows // 2
     f32 = jnp.float32
     wide = jax.ShapeDtypeStruct(weights.shape, f32)
     tiny = jax.ShapeDtypeStruct((1, MATS), f32)
     dma = pltpu.SemaphoreType.DMA
-    nw, nf, ns, low, wn, un, tr = pl.pallas_call(
+    result = (
+        wide, wide, wide,
+        jax.ShapeDtypeStruct((1, slots, depth * rows, width), jnp.bfloat16),
+        tiny, tiny, tiny,
+    )
+    held = pl.pallas_call(
         functools.partial(kernel, owns, rows),
-        out_shape=(
-            wide, wide, wide,
-            jax.ShapeDtypeStruct((1, slots, depth * rows, width), jnp.bfloat16),
-            tiny, tiny, tiny,
-        ),
-        in_specs=[any_space] * 4 + [vmem],
-        out_specs=(any_space,) * 4 + (vmem,) * 3,
+        out_shape=result,
+        in_specs=[hbm] * 5,
+        out_specs=(vmem,) * 7,
         scratch_shapes=[
             pltpu.VMEM((slots, depth, width), f32),
             pltpu.VMEM((slots, depth, width), f32),
             pltpu.VMEM((slots, depth, width), f32),
             pltpu.VMEM((slots, depth, width), jnp.bfloat16),
             pltpu.VMEM((slots, depth, width), f32),
-            pltpu.VMEM((slots, depth * rows, width), jnp.bfloat16),
+            pltpu.VMEM((1, owner.shape[0]), jnp.int32),
             pltpu.VMEM((slots, CHUNK), f32),
             pltpu.VMEM((slots, CHUNK), f32),
             pltpu.VMEM((slots, 8, 128), f32),
@@ -284,8 +281,7 @@
             pltpu.VMEM((owns, 1, 128), f32),
             pltpu.VMEM((rows, 1, 128), f32),
             dma((4, slots)),
-            dma((3, slots)),
-            dma((2, far + 1, slots)),
+            dma,
             dma((2,)),
             dma((2,)),
             dma((far, slots)),
@@ -296,7 +292,15 @@
         compiler_params=pltpu.CompilerParams(
             collective_id=0, has_side_effects=True, vmem_limit_bytes=24 << 20
         ),
-    )(weights, first_moment, second_moment, gradient, owner.reshape(1, -1))
+    )(*(pltpu.with_memory_space_constraint(x, pltpu.HBM) for x in (weights, first_moment, second_moment, gradient, owner.reshape(1, -1))))
+    nw, nf, ns, low, wn, un, tr = pl.pallas_call(
+        put_out,
+        out_shape=result,
+        in_specs=[vmem] * 7,
+        out_specs=(hbm,) * 7,
+        scratch_shapes=[dma((slots + 9,))],
+        compiler_params=pltpu.CompilerParams(vmem_limit_bytes=24 << 20),
+    )(*held)
     return nw, nf, ns, low, wn.reshape(MATS), un.reshape(MATS), tr.reshape(MATS)
 
 

time: 82.5 us -> 65.7 us (0.80)
  local copies, waits for them, and re-layouts: 11.8 us -> 0 us
  Pallas kernels: 69.7 us -> 65 us
    unnamed x17 -> x0, local copies, waits for them, and re-layouts: 11.8 us -> none
    pallas_call x1 -> x2, Pallas kernels: 69.7 us -> 65 us  [the longest x1 61.9 us: shards(): pl.pallas_call(functools.partial(kernel, owns, rows), out_shape=result, i...]
where the time goes in v2:
time: 65.7 us; the launch traced here: 65.6 us
  Pallas kernels  65 us (99%)
    pallas_call x1, Pallas kernels, shards(): pl.pallas_call(functools.partial(kernel, owns, rows), out_shape=result, i...  61.9 us
    pallas_call x1, Pallas kernels, shards(): pl.pallas_call(put_out, out_shape=result, in_specs=[vmem] * 7, out_specs=...  3.12 us

profile of v2, /device:TPU:2, one launch (start us, length us, event | category | flops | bytes accessed | tf_op | source)
XLA Modules:
  0.0 65.6 jit_solution(7883076177958515023)
XLA Ops:
  0.6 61.9 %shard_map.108 = (f32[1,8,16,2048]{3,2,1,0:T(8,128)S(1)}, f32[1,8,16,2048]{3,2,1,0:T(8,128)S(1)}, f32[1,8,16,2048]{3,2,1,0:T(8,128)S(1)}, bf16[1,8,128,2048]{3,2...) custom-call(f32[1,8,16,2048]{3,2,1,0:T(8,128)} %w_hbm.1, ...), custom_call_target="tpu_custom_call" | custom-call | tf_op jit(solution)/shard_map/pallas_call | solution.py:265
  62.5 3.1 %shard_map.109 = (f32[1,8,16,2048]{3,2,1,0:T(8,128)}, f32[1,8,16,2048]{3,2,1,0:T(8,128)}, f32[1,8,16,2048]{3,2,1,0:T(8,128)}, bf16[1,8,128,2048]{3,2,1,0:T(8,128...) custom-call(f32[1,8,16,2048]{3,2,1,0:T(8,128)S(1)} %get-tuple-element.21.refs_0_, ...), custom_call_target="tpu_custom_call" | custom-call | tf_op jit(solution)/shard_map/pallas_call | solution.py:296

commit v3 on v2

--- a/solution.py
+++ b/solution.py
@@ -62,8 +62,22 @@
     return out
 
 
+def pick_plan(plans, owns, owner_ref, plan_ref):
+    tiles = owner_ref.shape[1]
+    group = lax.broadcasted_iota(jnp.int32, (owns, tiles), 0)
+    hit = (jnp.broadcast_to(owner_ref[...], (owns, tiles)) == group).astype(jnp.float32)
+    counts = jnp.broadcast_to(jnp.sum(hit, axis=1, keepdims=True), (owns, 128))
+    odd = lax.broadcasted_iota(jnp.int32, (owns, 128), 0) % 2 == 1
+    most_even = jnp.max(jnp.where(odd, 0.0, counts)).astype(jnp.int32)
+    most_odd = jnp.max(jnp.where(odd, counts, 0.0)).astype(jnp.int32)
+    plan = jnp.int32(0)
+    for i, (even, odd_slots) in enumerate(plans):
+        plan = jnp.where((most_even <= even) & (most_odd <= odd_slots), i, plan)
+    plan_ref[0] = plan
+
+
 def kernel(
-    owns, rows,
+    owns, rows, sent,
     w_hbm, f_hbm, s_hbm, g_hbm, owner_hbm,
     nw, nf, ns, low, wn_ref, un_ref, tr_ref,
     wv, fv, sv, gv, dv, owner_ref, used_b, ratio_b, sw, su, abuf, bbuf,
@@ -72,6 +86,8 @@
     own = lax.axis_index("own")
     z = lax.axis_index("row")
     slots, depth, width = wv.shape
+
+    count = sent[0] + (sent[1] - sent[0]) * lax.rem(own, 2)
 
     barrier = pltpu.get_barrier_semaphore()
 
@@ -151,6 +167,10 @@
     def _(p):
         plane(p).start()
 
+    @pl.loop(count, slots)
+    def _(c):
+        low[0, c] = jnp.zeros(low.shape[2:], low.dtype)
+
     whole = abuf.at[pl.ds(0, owns - 1)]
     pltpu.make_async_copy(whole, whole, a_sem.at[1]).wait()
     total = jnp.sum(abuf[...], axis=0)
@@ -173,10 +193,17 @@
     ratio_b[...] = jnp.broadcast_to(STEP_SIZE * ratio, ratio_b.shape)
 
     right, left = lax.rem(z + 1, rows), lax.rem(z + rows - 1, rows)
+    far = rows // 2
+
+    def piece(c, src, h, to_right):
+        block = low.at[0, c, pl.ds(pl.multiple_of(src * depth, depth), depth)]
+        if h < far - 1:
+            return block
+        return block.at[:, pl.ds(0 if to_right else width // 2, width // 2)]
 
     def hop(c, h, to_right):
         src = lax.rem(z + rows - h, rows) if to_right else lax.rem(z + h, rows)
-        block = low.at[0, c, pl.ds(pl.multiple_of(src * depth, depth), depth)]
+        block = piece(c, src, h, to_right)
         send, recv = (rs_sem, rr_sem) if to_right else (ls_sem, lr_sem)
         return pltpu.make_async_remote_copy(
             src_ref=block, dst_ref=block,
@@ -186,7 +213,7 @@
 
     def arrival(c, h, to_right):
         src = lax.rem(z + rows - h - 1, rows) if to_right else lax.rem(z + h + 1, rows)
-        block = low.at[0, c, pl.ds(pl.multiple_of(src * depth, depth), depth)]
+        block = piece(c, src, h, to_right)
         recv = rr_sem if to_right else lr_sem
         pltpu.make_async_copy(block, block, recv.at[h, c]).wait()
 
@@ -201,29 +228,24 @@
             new = keep * (wv[c, :, cols] - rate * dv[c, :, cols])
             nw[0, c, :, cols] = new
             low[0, c, pl.ds(mine, depth), cols] = new.astype(jnp.bfloat16)
-        hop(c, 0, True).start()
-        hop(c, 0, False).start()
-
-    half = slots // 2
-    far = rows // 2
+
+        @pl.when(c < count)
+        def _():
+            hop(c, 0, True).start()
+            hop(c, 0, False).start()
+
     for h in range(far):
-        last = h == far - 1
-        for to_right, lo, hi in ((True, 0, half if last else slots), (False, half if last else 0, slots)):
-            @pl.loop(lo, hi)
-            def _(c):
+        @pl.loop(0, count)
+        def _(c):
+            for to_right in (True, False):
                 arrival(c, h, to_right)
-                if h + 1 < far - 1:
+                if h + 1 < far:
                     hop(c, h + 1, to_right).start()
-                elif h + 1 == far - 1:
-                    @pl.when((c < half) if to_right else (c >= half))
-                    def _():
-                        hop(c, h + 1, to_right).start()
 
     for h in range(far):
-        last = h == far - 1
-        for to_right, lo, hi in ((True, 0, half if last else slots), (False, half if last else 0, slots)):
-            @pl.loop(lo, hi)
-            def _(c):
+        @pl.loop(0, count)
+        def _(c):
+            for to_right in (True, False):
                 hop(c, h, to_right).wait_send()
 
     pltpu.make_async_copy(whole_b, whole_b, b_sem.at[0]).wait()
@@ -248,7 +270,7 @@
         copy.wait()
 
 
-def shards(owns, rows, weights, first_moment, second_moment, gradient, owner):
+def update(owns, rows, number, sent, weights, first_moment, second_moment, gradient, owner):
     _, slots, depth, width = weights.shape
     hbm = pl.BlockSpec(memory_space=pltpu.HBM)
     vmem = pl.BlockSpec(memory_space=pltpu.VMEM)
@@ -263,7 +285,7 @@
         tiny, tiny, tiny,
     )
     held = pl.pallas_call(
-        functools.partial(kernel, owns, rows),
+        functools.partial(kernel, owns, rows, sent),
         out_shape=result,
         in_specs=[hbm] * 5,
         out_specs=(vmem,) * 7,
@@ -290,7 +312,7 @@
             dma((far, slots)),
         ],
         compiler_params=pltpu.CompilerParams(
-            collective_id=0, has_side_effects=True, vmem_limit_bytes=24 << 20
+            collective_id=number, has_side_effects=True, vmem_limit_bytes=24 << 20
         ),
     )(*(pltpu.with_memory_space_constraint(x, pltpu.HBM) for x in (weights, first_moment, second_moment, gradient, owner.reshape(1, -1))))
     nw, nf, ns, low, wn, un, tr = pl.pallas_call(
@@ -304,6 +326,19 @@
     return nw, nf, ns, low, wn.reshape(MATS), un.reshape(MATS), tr.reshape(MATS)
 
 
+def shards(owns, rows, *arrays):
+    slots, owner = arrays[0].shape[1], arrays[-1]
+    plans = [(slots, slots), (slots, slots // 2), (slots // 2, slots)]
+    plan = pl.pallas_call(
+        functools.partial(pick_plan, plans, owns),
+        out_shape=jax.ShapeDtypeStruct((1,), jnp.int32),
+        in_specs=[pl.BlockSpec(memory_space=pltpu.VMEM)],
+        out_specs=pl.BlockSpec(memory_space=pltpu.SMEM),
+    )(owner.reshape(1, -1))
+    branches = [functools.partial(update, owns, rows, i, sent) for i, sent in enumerate(plans)]
+    return lax.switch(plan[0], branches, *arrays)
+
+
 def solution(mesh):
     placed = P("own", None, "row", None)
     return jax.shard_map(

time: 65.7 us -> 58.4 us (0.89); the launches traced: 65.6 us -> 57.5 us
  Pallas kernels: 65 us -> 56.2 us
    pallas_call x2 -> x3, Pallas kernels: 65 us -> 56.2 us  [the longest x1 51.8 us: update(): pl.pallas_call(functools.partial(kernel, owns, rows, sent), out_shape=res...]
where the time goes in v3:
time: 58.4 us; the launch traced here: 57.5 us
  Pallas kernels  56.2 us (96%)
  between operations  1.29 us (2%)
    pallas_call x1, Pallas kernels, update(): pl.pallas_call(functools.partial(kernel, owns, rows, sent), out_shape=res...  51.8 us
    pallas_call x1, Pallas kernels, update(): pl.pallas_call(put_out, out_shape=result, in_specs=[vmem] * 7, out_specs=...  3.12 us
    pallas_call x1, Pallas kernels, shards(): pl.pallas_call(functools.partial(pick_plan, plans, owns), out_shape=jax.S...  1.3 us

profile of v3, /device:TPU:2, one launch (start us, length us, event | category | flops | bytes accessed | tf_op | source)
XLA Modules:
  0.0 57.5 jit_solution(17815422930427303898)
XLA Ops:
  0.6 1.3 %shard_map.108 = s32[1]{0:T(128)} custom-call(s32[1,127]{1,0:T(1,128)} %bitcast.8), custom_call_target="tpu_custom_call" | custom-call | tf_op jit(solution)/shard_map/pallas_call | solution.py:332
  2.6 54.9 %conditional.1 = ((f32[1,8,16,2048]{3,2,1,0:T(8,128)}, f32[1,8,16,2048]{3,2,1,0:T(8,128)}, f32[1,8,16,2048]{3,2,1,0:T(8,128)}, bf16[1,8,128,2048]{3,2,1,0:T(8,12...) conditional(s32[]{:T(128)} %bitcast.1, (s32[127]{0:T(128)}, ...), branch_computations={%region_0.0_spmd.clone, %region_1.0_spmd.clone, %region_2.0_spmd.c... | conditional | bytes 8 | solution.py:339
  2.6 51.8 %branch_1_fun.2 = (f32[1,8,16,2048]{3,2,1,0:T(8,128)S(1)}, f32[1,8,16,2048]{3,2,1,0:T(8,128)S(1)}, f32[1,8,16,2048]{3,2,1,0:T(8,128)S(1)}, bf16[1,8,128,2048]{3,...) custom-call(f32[1,8,16,2048]{3,2,1,0:T(8,128)} %get-tuple-element.116.w_hbm, ...), custom_call_target="tpu_custom_call" | custom-call | tf_op jit(solution)/shard_map/cond/branch_1_fun/pallas_call | solution.py:287
  54.4 3.1 %branch_1_fun.3 = (f32[1,8,16,2048]{3,2,1,0:T(8,128)}, f32[1,8,16,2048]{3,2,1,0:T(8,128)}, f32[1,8,16,2048]{3,2,1,0:T(8,128)}, bf16[1,8,128,2048]{3,2,1,0:T(8,12...) custom-call(f32[1,8,16,2048]{3,2,1,0:T(8,128)S(1)} %get-tuple-element.121.refs_0_, ...), custom_call_target="tpu_custom_call" | custom-call | tf_op jit(solution)/shard_map/cond/branch_1_fun/pallas_call | solution.py:318

commit v4 on v3

--- a/solution.py
+++ b/solution.py
@@ -175,7 +175,6 @@
     pltpu.make_async_copy(whole, whole, a_sem.at[1]).wait()
     total = jnp.sum(abuf[...], axis=0)
     bbuf[pl.ds(z, 1)] = total.reshape(1, 1, 128)
-    pltpu.make_async_copy(whole, whole, a_sem.at[0]).wait()
 
     @pl.loop(1, rows)
     def _(p):
@@ -248,6 +247,7 @@
             for to_right in (True, False):
                 hop(c, h, to_right).wait_send()
 
+    pltpu.make_async_copy(whole, whole, a_sem.at[0]).wait()
     pltpu.make_async_copy(whole_b, whole_b, b_sem.at[0]).wait()
 
 

time: 58.4 us -> 57.6 us (0.986); the launches traced: 57.5 us -> 57.5 us
  no operation moved by 1% of the time
where the time goes in v4:
time: 57.6 us; the launch traced here: 57.5 us
  Pallas kernels  56.2 us (98%)
  between operations  1.29 us (2%)
    pallas_call x1, Pallas kernels, update(): pl.pallas_call(functools.partial(kernel, owns, rows, sent), out_shape=res...  51.8 us
    pallas_call x1, Pallas kernels, update(): pl.pallas_call(put_out, out_shape=result, in_specs=[vmem] * 7, out_specs=...  3.12 us
    pallas_call x1, Pallas kernels, shards(): pl.pallas_call(functools.partial(pick_plan, plans, owns), out_shape=jax.S...  1.3 us

profile of v4, /device:TPU:2, one launch (start us, length us, event | category | flops | bytes accessed | tf_op | source)
XLA Modules:
  0.0 57.5 jit_solution(11934034213261865636)
XLA Ops:
  0.6 1.3 %shard_map.108 = s32[1]{0:T(128)} custom-call(s32[1,127]{1,0:T(1,128)} %bitcast.8), custom_call_target="tpu_custom_call" | custom-call | tf_op jit(solution)/shard_map/pallas_call | solution.py:332
  2.6 54.9 %conditional.1 = ((f32[1,8,16,2048]{3,2,1,0:T(8,128)}, f32[1,8,16,2048]{3,2,1,0:T(8,128)}, f32[1,8,16,2048]{3,2,1,0:T(8,128)}, bf16[1,8,128,2048]{3,2,1,0:T(8,12...) conditional(s32[]{:T(128)} %bitcast.1, (s32[127]{0:T(128)}, ...), branch_computations={%region_0.0_spmd.clone, %region_1.0_spmd.clone, %region_2.0_spmd.c... | conditional | bytes 8 | solution.py:339
  2.6 51.8 %branch_1_fun.2 = (f32[1,8,16,2048]{3,2,1,0:T(8,128)S(1)}, f32[1,8,16,2048]{3,2,1,0:T(8,128)S(1)}, f32[1,8,16,2048]{3,2,1,0:T(8,128)S(1)}, bf16[1,8,128,2048]{3,...) custom-call(f32[1,8,16,2048]{3,2,1,0:T(8,128)} %get-tuple-element.116.w_hbm, ...), custom_call_target="tpu_custom_call" | custom-call | tf_op jit(solution)/shard_map/cond/branch_1_fun/pallas_call | solution.py:287
  54.4 3.1 %branch_1_fun.3 = (f32[1,8,16,2048]{3,2,1,0:T(8,128)}, f32[1,8,16,2048]{3,2,1,0:T(8,128)}, f32[1,8,16,2048]{3,2,1,0:T(8,128)}, bf16[1,8,128,2048]{3,2,1,0:T(8,12...) custom-call(f32[1,8,16,2048]{3,2,1,0:T(8,128)S(1)} %get-tuple-element.121.refs_0_, ...), custom_call_target="tpu_custom_call" | custom-call | tf_op jit(solution)/shard_map/cond/branch_1_fun/pallas_call | solution.py:318
